TPU v7x, 32 devices: a whole 2x2x4 slice. The times are simulated.
32 devices in a mesh: vp: 8 (over z, x), ch: 4 (over y, core).
Axes of the slice: x: 2, y: 2, z: 4, core: 2. Of those that a mesh axis runs over, the one named last changes fastest.
Arguments:
- chol_a: bfloat16 [640, 4, 6000], P('vp', None, 'ch'), may hold values from -0.078125 to 0.078125
- chol_b: bfloat16 [6000, 8, 640], P('ch', 'vp'), may hold values from -6 to 6
- amplitudes: bfloat16 [640, 8, 640], P('vp'), may hold values from -0.0390625 to 0.0390625
- vir_a: float32 [4], replicated, may hold values from 0.2 to 3
- vir_b: float32 [8], P('vp'), may hold values from 0.2 to 3
- occ_pair: float32 [8], P('ch'), may hold values from -4 to -1
Outputs:
- increment: float32 [4, 8, 8], P(None, 'vp', 'ch')
All inputs are finite; a program needn't handle non-finite values.
Results may differ from a plain program's by a relative error of at most 0.0029.
Values may be sent and summed in bfloat16 or wider, within the bound.
No kernel may reach another device: no remote copies, remote signals or barrier semaphores. Data moves between devices by JAX's collectives and lax.ppermute only.
A program may use at most 64 MiB of HBM per device.

v0:
```python
import jax
import jax.numpy as jnp
from jax import lax
from jax.sharding import PartitionSpec as P


def body(chol_a, chol_b, amplitudes, vir_a, vir_b, occ_pair):
    nch_dev = chol_b.shape[0]
    nb_dev = chol_b.shape[1]
    vir_count = chol_b.shape[2]
    a_count = chol_a.shape[1]
    pair_count = amplitudes.shape[1]
    cholesky_right = chol_b.reshape(nch_dev, nb_dev * vir_count)
    panel_rows = lax.all_gather(chol_a, "vp", axis=0, tiled=True)
    rows_here = panel_rows.shape[0]
    v_rows = jnp.dot(
        panel_rows.reshape(rows_here * a_count, nch_dev),
        cholesky_right,
        preferred_element_type=jnp.float32,
    )
    v_all = v_rows.astype(jnp.bfloat16).reshape(rows_here, a_count * nb_dev, vir_count)
    quarter = pair_count // lax.axis_size("ch")
    own_pairs = lax.dynamic_slice_in_dim(amplitudes, lax.axis_index("ch") * quarter, quarter, 1)
    spread = lax.all_gather(own_pairs, "vp", axis=0, tiled=True)
    all_pairs = lax.all_gather(spread, "ch", axis=1, tiled=True)
    ladder = jnp.einsum("cxd,cid->xi", v_all, all_pairs, preferred_element_type=jnp.float32)
    ladder = ladder.reshape(a_count, nb_dev, pair_count)
    ladder = lax.psum_scatter(ladder, "ch", scatter_dimension=2, tiled=True)
    energy_gap = vir_a[:, None, None] + vir_b[None, :, None] - occ_pair[None, None, :]
    return ladder / energy_gap


def solution(mesh):
    return jax.shard_map(
        body,
        mesh=mesh,
        in_specs=(
            P("vp", None, "ch"),
            P("ch", "vp", None),
            P("vp", None, None),
            P(),
            P("vp"),
            P("ch"),
        ),
        out_specs=P(None, "vp", "ch"),
        check_vma=False,
    )
```

profile of v0, /device:TPU:0, one launch (start us, length us, event | category | flops | bytes accessed | tf_op | source)
XLA Modules:
  0.0 245.8 jit_solution(5086026645808385693)
XLA Ops:
  6.5 0.0 copy-start
  6.5 0.0 all-gather.6.cloned.1.call-start
  6.5 0.0 copy-start.3
  6.5 0.0 copy-start.2
  6.5 2.2 constant_dynamic-slice_fusion.1
  8.7 0.0 all-gather.6.cloned.1.call-update
  8.8 0.0 all-gather.4.cloned.1.call-start
  8.8 0.7 all-gather.4.cloned.1.call-update
  9.5 0.0 all-gather.8.cloned.1.call-start
  9.6 47.5 %all-gather.6.cloned.1.call-done = bf16[640,2,640]{2,1,0:T(2,128)(2,1)} async-done(((bf16[80,2,640]{2,1,0:T(2,128)(2,1)}), bf16[640,2,640]{2,1,0:T(2,128)(2,1)}) %all-gather.6.cloned.1.call-update) | async-done | bytes 1638416 | tf_op jit(solution)/shard_map/all_gather | solution.py:24
  57.1 2.8 %copy.13 = bf16[640,2,640]{2,0,1:T(8,128)(2,1)} copy(bf16[640,2,640]{2,1,0:T(2,128)(2,1)} %all-gather.6.cloned.1.call-done) | data formatting | bytes 3276800 | tf_op jit(solution)/shard_map/all_gather | solution.py:24
  59.9 0.0 all-gather.8.cloned.1.call-update
  60.6 0.0 copy-done.3
  60.6 0.6 dynamic-slice
  61.8 0.0 copy-done.2
  61.9 113.8 %all-gather.4.cloned.1.call-done = bf16[640,4,1500]{2,1,0:T(4,128)(2,1)} async-done(((bf16[80,4,1500]{2,1,0:T(4,128)(2,1)}), bf16[640,4,1500]{2,1,0:T(4,128)(2,1)}) %all-gather.4.cloned.1.call-update) | async-done | bytes 7680016 | tf_op jit(solution)/shard_map/all_gather | solution.py:14
  175.6 13.5 %reshape.60 = bf16[2560,1500]{1,0:T(8,128)(2,1)} reshape(bf16[640,4,1500]{2,1,0:T(4,128)(2,1)} %all-gather.4.cloned.1.call-done) | data formatting | bytes 15360000 | tf_op jit(solution)/shard_map/reshape | solution.py:17
  189.1 0.0 copy-done
  189.1 9.8 %convolution_convert_fusion = bf16[2560,640]{1,0:T(8,128)(2,1)} fusion(bf16[2560,1500]{1,0:T(8,128)(2,1)} %reshape.60, bf16[1500,1,640]{2,0,1:T(8,128)(2,1)S(1)} %copy-done), kind=kOutput, calls=%fused_computation.2 | convolution fusion | flops 4916838400 | bytes 12876800 | tf_op jit(solution)/shard_map/dot_general | solution.py:16
  198.9 6.5 %reshape.62 = bf16[640,4,640]{2,1,0:T(4,128)(2,1)} reshape(bf16[2560,640]{1,0:T(8,128)(2,1)} %convolution_convert_fusion) | data formatting | bytes 6553600 | tf_op jit(solution)/shard_map/reshape | solution.py:21
  205.4 0.0 copy-start.1
  205.4 17.9 %all-gather.8.cloned.1.call-done = bf16[640,8,640]{2,0,1:T(8,128)(2,1)} async-done(((bf16[640,2,640]{2,0,1:T(8,128)(2,1)}), bf16[640,8,640]{2,0,1:T(8,128)(2,1)}) %all-gather.8.cloned.1.call-update) | async-done | bytes 6553616 | tf_op jit(solution)/shard_map/all_gather | solution.py:25
  223.3 9.5 %fusion = f32[4,8,1]{0,1,2:T(8,128)S(1)} fusion(bf16[640,4,640]{2,1,0:T(4,128)(2,1)} %reshape.62, bf16[640,8,640]{2,0,1:T(8,128)(2,1)} %all-gather.8.cloned.1.call-done), kind=kOutput, calls=%fused_computation | convolution fusion | flops 26214400 | bytes 9830528 | tf_op jit(solution)/shard_map/cxd,cid->xi/dot_general | solution.py:26
  232.7 5.9 %all-reduce = f32[4,1,8]{0,1,2:T(1,128)S(1)} all-reduce(f32[4,1,8]{0,1,2:T(1,128)S(1)} %bitcast.13), channel_id=2, replica_groups=mesh['vp'=8,'ch'=4] {'ch'}, use_global_device_ids=true, to_apply=%region_0.0.clone | all-reduce | flops 32 | bytes 256
  238.6 0.0 copy-done.1
  238.6 0.6 subtract_divide_fusion
  (2 shorter events, 0.0 us)
Async XLA Ops:
  6.5 182.5 %copy-start = (bf16[1500,1,640]{2,0,1:T(8,128)(2,1)S(1)}, bf16[1500,1,640]{2,0,1:T(8,128)(2,1)}, u32[]{:S(2)}) copy-start(bf16[1500,1,640]{2,0,1:T(8,128)(2,1)} %param.7) | copy-start | bytes 5760004
  6.5 50.6 %all-gather.6.cloned.1.call-start = ((), (), s32[]{:S(2)}) async-start(), calls=%async_computation.1 | async-start | bytes 1843200 | tf_op jit(solution)/shard_map/all_gather | solution.py:24
  6.5 54.1 %copy-start.3 = (u32[32]{0:T(128)S(1)}, u32[32]{0:T(128)}, u32[]{:S(2)}) copy-start(u32[32]{0:T(128)} %constant.15) | copy-start | bytes 388
  6.5 55.3 %copy-start.2 = (f32[4]{0:T(128)S(1)}, f32[4]{0:T(128)}, u32[]{:S(2)}) copy-start(f32[4]{0:T(128)} %param.9) | copy-start | bytes 52
  8.8 166.9 %all-gather.4.cloned.1.call-start = ((), (), s32[]{:S(2)}) async-start(), calls=%async_computation | async-start | bytes 8847360 | tf_op jit(solution)/shard_map/all_gather | solution.py:14
  9.5 213.7 %all-gather.8.cloned.1.call-start = ((), (), s32[]{:S(2)}) async-start(), calls=%async_computation.2 | async-start | bytes 8192000 | tf_op jit(solution)/shard_map/all_gather | solution.py:25
  205.4 33.3 %copy-start.1 = (f32[2]{0:T(128)S(1)}, f32[2]{0:T(128)}, u32[]{:S(2)}) copy-start(f32[2]{0:T(128)} %param.11) | copy-start | bytes 28
Sparse Core Ops, SparseCore 0:
  9.5 47.5 all-gather.5
  59.3 116.2 all-gather.3
  177.2 46.0 all-gather.7
where the time goes:
time: 246 us
  waiting for transfers between devices  180 us (73%)
  local copies, waits for them, and re-layouts  25.6 us (10%)
  matrix products  19.3 us (8%)
  between operations  14.4 us (6%)
  blocking collectives  5.89 us (2%)
    all_gather x1, waiting for transfers between devices, body(): panel_rows = lax.all_gather(chol_a, 'vp', axis=0, tiled=True)  114 us
    all_gather x1, waiting for transfers between devices, body(): spread = lax.all_gather(own_pairs, 'vp', axis=0, tiled=True)  47.5 us
    all_gather x1, waiting for transfers between devices, body(): all_pairs = lax.all_gather(spread, 'ch', axis=1, tiled=True)  17.9 us
    reshape x1, local copies, waits for them, and re-layouts, body(): panel_rows.reshape(rows_here * a_count, nch_dev)  13.5 us
    dot_general x1, matrix products, body(): jnp.dot(panel_rows.reshape(rows_here * a_count, nch_dev), cholesky_right,...  9.8 us
    dot_general x1, matrix products, body(): jnp.einsum('cxd,cid->xi', v_all, all_pairs, preferred_element_type=jnp.fl...  9.47 us
    reshape x1, local copies, waits for them, and re-layouts, body(): v_rows.astype(jnp.bfloat16).reshape(rows_here, a_count * nb_dev, vir_count)  6.49 us
    unnamed x1, blocking collectives  5.89 us
  transfers between devices with their start and end apart: 3, of which 3 were waited for; matrix products, arithmetic and copies ran while one was open for 13% of the time, Pallas kernels for 0%

commit v1 on v0

--- a/solution.py
+++ b/solution.py
@@ -1,7 +1,27 @@
+import functools
 import jax
 import jax.numpy as jnp
 from jax import lax
 from jax.sharding import PartitionSpec as P
+from jax.lax import axis_index, axis_size, ppermute
+
+
+def _update_sites(unit, which_dim):
+    n = axis_size("vp")
+    arr_out = range(1, n)
+    upper = map(lambda pp: (pp - 1, pp), arr_out)
+    val = list(upper)
+    b_now = val + [(n - 1, 0)]
+    fresh = unit
+    line_up = [fresh]
+    for _ in [*range(n - 1)]:
+        fresh = ppermute(fresh, "vp", b_now)
+        line_up += [fresh]
+    r2 = jnp.concatenate([*reversed(line_up)], axis=which_dim)
+    return jnp.roll(r2, (axis_index("vp") + 1) * fresh.shape[which_dim], which_dim)
+
+
+_remake_windows = functools.partial(_update_sites, which_dim=0)
 
 
 def body(chol_a, chol_b, amplitudes, vir_a, vir_b, occ_pair):
@@ -11,7 +31,7 @@
     a_count = chol_a.shape[1]
     pair_count = amplitudes.shape[1]
     cholesky_right = chol_b.reshape(nch_dev, nb_dev * vir_count)
-    panel_rows = lax.all_gather(chol_a, "vp", axis=0, tiled=True)
+    panel_rows = _remake_windows(chol_a)
     rows_here = panel_rows.shape[0]
     v_rows = jnp.dot(
         panel_rows.reshape(rows_here * a_count, nch_dev),

time: 246 us -> 296 us (1.20)
  local copies, waits for them, and re-layouts: 25.6 us -> 72.1 us
    ppermute x0 -> x7, waiting for transfers between devices: none -> 179 us  [_update_sites(): fresh = ppermute(fresh, 'vp', b_now)]
    all_gather x1 -> x0, waiting for transfers between devices: 114 us -> none  [body(): panel_rows = lax.all_gather(chol_a, 'vp', axis=0, tiled=True)]
    all_gather x1, waiting for transfers between devices: 47.5 us -> 0.01 us  [body(): spread = lax.all_gather(own_pairs, 'vp', axis=0, tiled=True)]
    unnamed x10 -> x31, local copies, waits for them, and re-layouts: 0.61 us -> 37.2 us
    all_gather x1, waiting for transfers between devices: 17.9 us -> 0.01 us  [body(): all_pairs = lax.all_gather(spread, 'ch', axis=1, tiled=True)]
    dynamic_slice x0 -> x1, local copies, waits for them, and re-layouts: none -> 9.08 us  [_update_sites(): jnp.roll(r2, (axis_index('vp') + 1) * fresh.shape[which_dim], which_dim)]
    ppermute x0 -> x7, starting transfers between devices: none -> 2.98 us  [_update_sites(): fresh = ppermute(fresh, 'vp', b_now)]
  transfers between devices with their start and end apart: 3 -> 9, of which waited for: 3 -> 7; matrix products, arithmetic and copies ran while one was open for 13% -> 27% of each run, Pallas kernels for 0% -> 0%
where the time goes in v1:
time: 296 us; the launch traced here: 295 us
  waiting for transfers between devices  179 us (60%)
  local copies, waits for them, and re-layouts  72.1 us (24%)
  matrix products  19.2 us (6%)
  between operations  14.8 us (5%)
  blocking collectives  5.89 us (2%)
  starting transfers between devices  3.03 us (1%)
    ppermute x7, waiting for transfers between devices, _update_sites(): fresh = ppermute(fresh, 'vp', b_now)  179 us
    unnamed x31, local copies, waits for them, and re-layouts  37.2 us
    reshape x1, local copies, waits for them, and re-layouts, body(): panel_rows.reshape(rows_here * a_count, nch_dev)  13.2 us
    dot_general x1, matrix products, body(): jnp.dot(panel_rows.reshape(rows_here * a_count, nch_dev), cholesky_right,...  9.74 us
    dot_general x1, matrix products, body(): jnp.einsum('cxd,cid->xi', v_all, all_pairs, preferred_element_type=jnp.fl...  9.47 us
    dynamic_slice x1, local copies, waits for them, and re-layouts, _update_sites(): jnp.roll(r2, (axis_index('vp') + 1) * fresh.shape[which_dim], which_dim)  9.08 us
    reshape x1, local copies, waits for them, and re-layouts, body(): v_rows.astype(jnp.bfloat16).reshape(rows_here, a_count * nb_dev, vir_count)  6.51 us
  transfers between devices with their start and end apart: 9, of which 7 were waited for; matrix products, arithmetic and copies ran while one was open for 27% of the time, Pallas kernels for 0%

profile of v1, /device:TPU:0, one launch (start us, length us, event | category | flops | bytes accessed | tf_op | source)
XLA Modules:
  0.0 295.2 jit_solution(8753736666226934506)
XLA Ops:
  6.5 0.0 copy-start
  6.5 0.0 copy-start.1
  6.5 0.0 all-gather.3.cloned.1.call-start
  6.5 3.0 %collective-permute-start = (bf16[80,4,1500]{2,1,0:T(4,128)(2,1)}, bf16[80,4,1500]{2,1,0:T(4,128)(2,1)}, u32[]{:S(2)}, u32[]{:S(2)}) collective-permute-start(bf16[80,4,1500]{2,1,0:T(4,128)(2,1)} %param.6), channel_id=1, source_target_pairs={{0,4},{4,8},{8,12},{12,16},{16,20},{20,24},{24,28},{28,0},{1,5},{5... | collective-permute-start | bytes 2880008 | tf_op jit(solution)/shard_map/ppermute | solution.py:18
  9.5 2.0 constant_dynamic-slice_fusion.1
  11.5 0.0 all-gather.3.cloned.1.call-update
  11.6 0.0 all-gather.5.cloned.1.call-start
  11.6 29.6 %collective-permute-done = bf16[80,4,1500]{2,1,0:T(4,128)(2,1)} collective-permute-done((bf16[80,4,1500]{2,1,0:T(4,128)(2,1)}, bf16[80,4,1500]{2,1,0:T(4,128)(2,1)}, u32[]{:S(2)}, u32[]{:S(2)}) %collective-permute-start) | collective-permute-done | bytes 960032 | tf_op jit(solution)/shard_map/ppermute | solution.py:18
  41.2 0.0 collective-permute-start.1
  41.2 39.1 %collective-permute-done.1 = bf16[80,4,1500]{2,1,0:T(4,128)(2,1)S(1)} collective-permute-done((bf16[80,4,1500]{2,1,0:T(4,128)(2,1)}, bf16[80,4,1500]{2,1,0:T(4,128)(2,1)S(1)}, u32[]{:S(2)}, u32[]{:S(2)}) %collective-permute-start.1) | collective-permute-done | bytes 960032 | tf_op jit(solution)/shard_map/ppermute | solution.py:18
  80.3 0.0 copy-start.2
  80.3 0.9 copy-done.2
  81.3 0.0 collective-permute-start.2
  81.3 24.9 %collective-permute-done.2 = bf16[80,4,1500]{2,1,0:T(4,128)(2,1)} collective-permute-done((bf16[80,4,1500]{2,1,0:T(4,128)(2,1)S(1)}, bf16[80,4,1500]{2,1,0:T(4,128)(2,1)}, u32[]{:S(2)}, u32[]{:S(2)}) %collective-permute-start.2) | collective-permute-done | bytes 960032 | tf_op jit(solution)/shard_map/ppermute | solution.py:18
  106.1 0.0 collective-permute-start.3
  106.1 0.0 all-gather.3.cloned.1.call-done
  106.1 2.8 copy.13
  108.9 0.0 all-gather.5.cloned.1.call-update
  109.0 21.4 %collective-permute-done.3 = bf16[80,4,1500]{2,1,0:T(4,128)(2,1)} collective-permute-done((bf16[80,4,1500]{2,1,0:T(4,128)(2,1)}, bf16[80,4,1500]{2,1,0:T(4,128)(2,1)}, u32[]{:S(2)}, u32[]{:S(2)}) %collective-permute-start.3) | collective-permute-done | bytes 960032 | tf_op jit(solution)/shard_map/ppermute | solution.py:18
  130.3 0.0 collective-permute-start.4
  130.3 23.3 %collective-permute-done.4 = bf16[80,4,1500]{2,1,0:T(4,128)(2,1)S(1)} collective-permute-done((bf16[80,4,1500]{2,1,0:T(4,128)(2,1)}, bf16[80,4,1500]{2,1,0:T(4,128)(2,1)S(1)}, u32[]{:S(2)}, u32[]{:S(2)}) %collective-permute-start.4) | collective-permute-done | bytes 960032 | tf_op jit(solution)/shard_map/ppermute | solution.py:18
  153.6 0.0 copy-start.4
  153.6 1.0 copy-done.4
  154.5 0.0 collective-permute-start.5
  154.6 22.3 %collective-permute-done.5 = bf16[80,4,1500]{2,1,0:T(4,128)(2,1)} collective-permute-done((bf16[80,4,1500]{2,1,0:T(4,128)(2,1)S(1)}, bf16[80,4,1500]{2,1,0:T(4,128)(2,1)}, u32[]{:S(2)}, u32[]{:S(2)}) %collective-permute-start.5) | collective-permute-done | bytes 960032 | tf_op jit(solution)/shard_map/ppermute | solution.py:18
  176.8 0.0 collective-permute-start.6
  177.5 1.2 dynamic-slice
  179.4 0.0 copy-start.5
  179.4 0.0 copy-start.3
  179.4 0.8 broadcast_add_fusion
  180.2 18.3 %collective-permute-done.6 = bf16[80,4,1500]{2,1,0:T(4,128)(2,1)} collective-permute-done((bf16[80,4,1500]{2,1,0:T(4,128)(2,1)}, bf16[80,4,1500]{2,1,0:T(4,128)(2,1)}, u32[]{:S(2)}, u32[]{:S(2)}) %collective-permute-start.6) | collective-permute-done | bytes 960032 | tf_op jit(solution)/shard_map/ppermute | solution.py:18
  198.5 2.5 constant_dynamic-update-slice_fusion.15
  201.0 2.5 constant_dynamic-update-slice_fusion.14
  203.5 2.5 constant_dynamic-update-slice_fusion.13
  206.0 2.5 constant_dynamic-update-slice_fusion.12
  208.5 2.5 constant_dynamic-update-slice_fusion.11
  211.0 2.5 constant_dynamic-update-slice_fusion.10
  213.5 2.5 constant_dynamic-update-slice_fusion.9
  216.0 0.0 copy-done.1
  216.0 1.3 constant_dynamic-update-slice_fusion.8
  217.3 2.6 constant_dynamic-update-slice_fusion.7
  219.9 2.5 constant_dynamic-update-slice_fusion.6
  222.3 0.0 copy-done.5
  222.3 1.3 constant_dynamic-update-slice_fusion.5
  223.6 2.5 constant_dynamic-update-slice_fusion.4
  226.1 2.5 constant_dynamic-update-slice_fusion.3
  228.7 0.0 copy-done.3
  228.7 1.4 constant_dynamic-update-slice_fusion.2
  230.0 2.5 constant_dynamic-update-slice_fusion.1
  232.5 1.3 constant_dynamic-update-slice_fusion
  233.8 9.1 %constant_dynamic-slice_fusion.2 = bf16[640,4,1500]{2,1,0:T(4,128)(2,1)} fusion(bf16[1280,4,1500]{2,1,0:T(4,128)(2,1)} %constant_dynamic-update-slice_fusion, s32[]{:T(128)S(6)} %select_n.17), kind=kLoop, calls=%fused_computation.23 | loop fusion | bytes 15360004 | tf_op jit(solution)/shard_map/jit(_roll_dynamic)/dynamic_slice | solution.py:21
  242.9 13.2 %reshape.60 = bf16[2560,1500]{1,0:T(8,128)(2,1)} reshape(bf16[640,4,1500]{2,1,0:T(4,128)(2,1)} %constant_dynamic-slice_fusion.2) | data formatting | bytes 15360000 | tf_op jit(solution)/shard_map/reshape | solution.py:37
  256.1 0.0 copy-done
  256.1 9.7 %convolution_convert_fusion = bf16[2560,640]{1,0:T(8,128)(2,1)} fusion(bf16[2560,1500]{1,0:T(8,128)(2,1)} %reshape.60, bf16[1500,1,640]{2,0,1:T(8,128)(2,1)S(1)} %copy-done), kind=kOutput, calls=%fused_computation.2 | convolution fusion | flops 4916838400 | bytes 12876800 | tf_op jit(solution)/shard_map/dot_general | solution.py:36
  265.9 0.0 copy-start.6
  265.9 6.5 %reshape.62 = bf16[640,4,640]{2,1,0:T(4,128)(2,1)} reshape(bf16[2560,640]{1,0:T(8,128)(2,1)} %convolution_convert_fusion) | data formatting | bytes 6553600 | tf_op jit(solution)/shard_map/reshape | solution.py:41
  272.4 0.0 all-gather.5.cloned.1.call-done
  272.4 9.5 %fusion = f32[4,8,1]{0,1,2:T(8,128)S(1)} fusion(bf16[640,4,640]{2,1,0:T(4,128)(2,1)} %reshape.62, bf16[640,8,640]{2,0,1:T(8,128)(2,1)} %all-gather.5.cloned.1.call-done), kind=kOutput, calls=%fused_computation | convolution fusion | flops 26214400 | bytes 9830528 | tf_op jit(solution)/shard_map/cxd,cid->xi/dot_general | solution.py:46
  281.8 5.9 %all-reduce = f32[4,1,8]{0,1,2:T(1,128)S(1)} all-reduce(f32[4,1,8]{0,1,2:T(1,128)S(1)} %bitcast.13), channel_id=2, replica_groups=mesh['vp'=8,'ch'=4] {'ch'}, use_global_device_ids=true, to_apply=%region_0.1.clone | all-reduce | flops 32 | bytes 256
  287.7 0.0 copy-done.6
  287.7 0.6 subtract_divide_fusion
  (1 shorter events, 0.0 us)
Async XLA Ops:
  6.5 249.6 %copy-start = (bf16[1500,1,640]{2,0,1:T(8,128)(2,1)S(1)}, bf16[1500,1,640]{2,0,1:T(8,128)(2,1)}, u32[]{:S(2)}) copy-start(bf16[1500,1,640]{2,0,1:T(8,128)(2,1)} %param.7) | copy-start | bytes 5760004
  6.5 209.5 %copy-start.1 = (bf16[80,4,1500]{2,1,0:T(4,128)(2,1)S(1)}, bf16[80,4,1500]{2,1,0:T(4,128)(2,1)}, u32[]{:S(2)}) copy-start(bf16[80,4,1500]{2,1,0:T(4,128)(2,1)} %param.6) | copy-start | bytes 2880004
  6.5 99.6 %all-gather.3.cloned.1.call-start = ((), (), s32[]{:S(2)}) async-start(), calls=%async_computation | async-start | bytes 1843200 | tf_op jit(solution)/shard_map/all_gather | solution.py:44
  6.5 34.7 %collective-permute-start = (bf16[80,4,1500]{2,1,0:T(4,128)(2,1)}, bf16[80,4,1500]{2,1,0:T(4,128)(2,1)}, u32[]{:S(2)}, u32[]{:S(2)}) collective-permute-start(bf16[80,4,1500]{2,1,0:T(4,128)(2,1)} %param.6), channel_id=1, source_target_pairs={{0,4},{4,8},{8,12},{12,16},{16,20},{20,24},{24,28},{28,0},{1,5},{5... | collective-permute-start | bytes 2880008 | tf_op jit(solution)/shard_map/ppermute | solution.py:18
  11.6 260.8 %all-gather.5.cloned.1.call-start = ((), (), s32[]{:S(2)}) async-start(), calls=%async_computation.1 | async-start | bytes 8192000 | tf_op jit(solution)/shard_map/all_gather | solution.py:45
  41.2 39.1 %collective-permute-start.1 = (bf16[80,4,1500]{2,1,0:T(4,128)(2,1)}, bf16[80,4,1500]{2,1,0:T(4,128)(2,1)S(1)}, u32[]{:S(2)}, u32[]{:S(2)}) collective-permute-start(bf16[80,4,1500]{2,1,0:T(4,128)(2,1)} %collective-permute-done), channel_id=1, source_target_pairs={{0,4},{4,8},{8,12},{12,16},{16,20},{20,24},{24,28},{28,0},{1,5},{5... | collective-permute-start | bytes 2880008 | tf_op jit(solution)/shard_map/ppermute | solution.py:18
  80.3 0.9 copy-start.2
  81.3 24.9 %collective-permute-start.2 = (bf16[80,4,1500]{2,1,0:T(4,128)(2,1)S(1)}, bf16[80,4,1500]{2,1,0:T(4,128)(2,1)}, u32[]{:S(2)}, u32[]{:S(2)}) collective-permute-start(bf16[80,4,1500]{2,1,0:T(4,128)(2,1)S(1)} %collective-permute-done.1), channel_id=1, source_target_pairs={{0,4},{4,8},{8,12},{12,16},{16,20},{20,24},{24,28},{28,0},{1,5},{5... | collective-permute-start | bytes 2880008 | tf_op jit(solution)/shard_map/ppermute | solution.py:18
  106.1 24.2 %collective-permute-start.3 = (bf16[80,4,1500]{2,1,0:T(4,128)(2,1)}, bf16[80,4,1500]{2,1,0:T(4,128)(2,1)}, u32[]{:S(2)}, u32[]{:S(2)}) collective-permute-start(bf16[80,4,1500]{2,1,0:T(4,128)(2,1)} %collective-permute-done.2), channel_id=1, source_target_pairs={{0,4},{4,8},{8,12},{12,16},{16,20},{20,24},{24,28},{28,0},{1,5},{5... | collective-permute-start | bytes 2880008 | tf_op jit(solution)/shard_map/ppermute | solution.py:18
  130.3 23.3 %collective-permute-start.4 = (bf16[80,4,1500]{2,1,0:T(4,128)(2,1)}, bf16[80,4,1500]{2,1,0:T(4,128)(2,1)S(1)}, u32[]{:S(2)}, u32[]{:S(2)}) collective-permute-start(bf16[80,4,1500]{2,1,0:T(4,128)(2,1)} %collective-permute-done.3), channel_id=1, source_target_pairs={{0,4},{4,8},{8,12},{12,16},{16,20},{20,24},{24,28},{28,0},{1,5},{5... | collective-permute-start | bytes 2880008 | tf_op jit(solution)/shard_map/ppermute | solution.py:18
  153.6 1.0 copy-start.4
  154.5 22.3 %collective-permute-start.5 = (bf16[80,4,1500]{2,1,0:T(4,128)(2,1)S(1)}, bf16[80,4,1500]{2,1,0:T(4,128)(2,1)}, u32[]{:S(2)}, u32[]{:S(2)}) collective-permute-start(bf16[80,4,1500]{2,1,0:T(4,128)(2,1)S(1)} %collective-permute-done.4), channel_id=1, source_target_pairs={{0,4},{4,8},{8,12},{12,16},{16,20},{20,24},{24,28},{28,0},{1,5},{5... | collective-permute-start | bytes 2880008 | tf_op jit(solution)/shard_map/ppermute | solution.py:18
  176.8 21.6 %collective-permute-start.6 = (bf16[80,4,1500]{2,1,0:T(4,128)(2,1)}, bf16[80,4,1500]{2,1,0:T(4,128)(2,1)}, u32[]{:S(2)}, u32[]{:S(2)}) collective-permute-start(bf16[80,4,1500]{2,1,0:T(4,128)(2,1)} %collective-permute-done.5), channel_id=1, source_target_pairs={{0,4},{4,8},{8,12},{12,16},{16,20},{20,24},{24,28},{28,0},{1,5},{5... | collective-permute-start | bytes 2880008 | tf_op jit(solution)/shard_map/ppermute | solution.py:18
  179.4 42.9 %copy-start.5 = (bf16[80,4,1500]{2,1,0:T(4,128)(2,1)S(1)}, bf16[80,4,1500]{2,1,0:T(4,128)(2,1)}, u32[]{:S(2)}) copy-start(bf16[80,4,1500]{2,1,0:T(4,128)(2,1)} %copy-done.4) | copy-start | bytes 2880004
  179.4 49.2 %copy-start.3 = (bf16[80,4,1500]{2,1,0:T(4,128)(2,1)S(1)}, bf16[80,4,1500]{2,1,0:T(4,128)(2,1)}, u32[]{:S(2)}) copy-start(bf16[80,4,1500]{2,1,0:T(4,128)(2,1)} %copy-done.2) | copy-start | bytes 2880004
  265.9 21.9 %copy-start.6 = (f32[2]{0:T(128)S(1)}, f32[2]{0:T(128)}, u32[]{:S(2)}) copy-start(f32[2]{0:T(128)} %param.11) | copy-start | bytes 28
Sparse Core Ops, SparseCore 0:
  11.7 60.1 all-gather.2
  109.1 48.9 all-gather.4
